TPU v7x, 32 devices: a whole 2x2x4 slice. The times are simulated.
32 devices in a mesh: dp: 4 (over y, core), tensor: 8 (over z, x).
Axes of the slice: x: 2, y: 2, z: 4, core: 2. Of those that a mesh axis runs over, the one named last changes fastest.
Arguments:
- tokens: bfloat16 [8192, 2048], P(('dp', 'tensor')), may hold values from -6 to 6
- gain_one: float32 [2048], replicated, may hold values from 0.5 to 1.5
- w_query: bfloat16 [2048, 256], P(None, 'tensor'), may hold values from -0.125 to 0.125
- w_key: bfloat16 [2048, 256], P(None, 'tensor'), may hold values from -0.125 to 0.125
- w_value: bfloat16 [2048, 2048], P(None, 'tensor'), may hold values from -0.125 to 0.125
- w_out: bfloat16 [2048, 2048], P('tensor'), may hold values from -0.5 to 0.5
- gain_two: float32 [2048], replicated, may hold values from 0.5 to 1.5
- w_gate: bfloat16 [2048, 5632], P(None, 'tensor'), may hold values from -0.125 to 0.125
- w_up: bfloat16 [2048, 5632], P(None, 'tensor'), may hold values from -0.125 to 0.125
- w_down: bfloat16 [5632, 2048], P('tensor'), may hold values from -0.078125 to 0.078125
- doc_ids: int32 [4, 2048], P('dp'), may hold values from 0 to 7, never falling along the last dimension, each value on 1 to 1024 neighbouring positions
- cotangent: bfloat16 [8192, 2048], P(('dp', 'tensor')), may hold values from -6 to 6
Outputs:
- block_out: bfloat16 [8192, 2048], P(('dp', 'tensor'))
- grad_tokens: float32 [8192, 2048], P(('dp', 'tensor'))
- grad_gain_one: float32 [2048], replicated
- grad_query: float32 [2048, 256], P(None, 'tensor')
- grad_key: float32 [2048, 256], P(None, 'tensor')
- grad_value: float32 [2048, 2048], P(None, 'tensor')
- grad_out_proj: float32 [2048, 2048], P('tensor')
- grad_gain_two: float32 [2048], replicated
- grad_gate: float32 [2048, 5632], P(None, 'tensor')
- grad_up: float32 [2048, 5632], P(None, 'tensor')
- grad_down: float32 [5632, 2048], P('tensor')
Inputs may be any that keep to these rules, and one draw needn't show every extreme that they name: Each row of doc_ids never falls along the row; each of the 8 documents of a group has 1 to 1024 tokens, and one has exactly 1024.
All inputs are finite; a program needn't handle non-finite values.
Results may differ from a plain program's by a relative error of at most 0.02.
Values may be sent and summed in bfloat16 or wider, within the bound.
No kernel may reach another device: no remote copies, remote signals or barrier semaphores. Data moves between devices by JAX's collectives and lax.ppermute only.
A program may use at most 256 MiB of HBM per device.

v0:
```python
import jax
import jax.numpy as jnp
from jax import lax
from jax.sharding import PartitionSpec as P

FEAT = 16
HEAD_V = 128
EPS = 1e-05


def norm_rows(values, gain_vec):
    row_scale = lax.rsqrt(jnp.mean(values * values, axis=-1, keepdims=True) + EPS)
    normed = values * row_scale
    return (normed, row_scale, (normed * gain_vec).astype(jnp.bfloat16))


def norm_back(grad_normed, normed, row_scale, gain_vec):
    weighted = grad_normed * gain_vec
    inner_mean = jnp.mean(weighted * normed, axis=-1, keepdims=True)
    return (row_scale * (weighted - normed * inner_mean), jnp.sum(grad_normed * normed, axis=0))


def contract_rows(left_mat, right_mat):
    return lax.dot_general(
        left_mat, right_mat, (((0,), (0,)), ((), ())), preferred_element_type=jnp.float32
    )


def times_transposed(left_mat, right_mat):
    return lax.dot_general(
        left_mat, right_mat, (((1,), (1,)), ((), ())), preferred_element_type=jnp.float32
    )


def block_kernel(query_rows, key_row_block, doc_row, row_start, block_rows):
    row_end_index = row_start + block_rows
    query_portion = query_rows[row_start:row_end_index]
    score_matrix = (
        jnp.einsum(
            "gsn,jsn->sgj",
            query_portion,
            key_row_block[:row_end_index],
            preferred_element_type=jnp.float32,
        )
        * 0.25
    )
    query_index = row_start + jnp.arange(block_rows)
    key_index = jnp.arange(row_end_index)
    allowed = (doc_row[row_start:row_end_index, None] == doc_row[None, :row_end_index]) & (
        query_index[:, None] >= key_index[None, :]
    )
    kernel = jnp.where(allowed[None], 1.0 + score_matrix + 0.5 * score_matrix * score_matrix, 0.0)
    return (score_matrix, allowed, kernel)


def attention_forward(query_rows, key_row_block, value_rows, doc_row, block_rows):
    group_rows = query_rows.shape[0]
    outputs = []
    denoms = []
    for row_start in range(0, group_rows, block_rows):
        row_end_index = row_start + block_rows
        score_matrix, allowed, kernel = block_kernel(
            query_rows, key_row_block, doc_row, row_start, block_rows
        )
        denominator = jnp.sum(kernel, axis=-1)
        numerator = jnp.einsum(
            "hqk,khd->qhd",
            kernel.astype(jnp.bfloat16),
            value_rows[:row_end_index],
            preferred_element_type=jnp.float32,
        )
        outputs.append((numerator / denominator.T[:, :, None]).astype(jnp.bfloat16))
        denoms.append(denominator)
    return (jnp.concatenate(outputs, axis=0), jnp.concatenate(denoms, axis=1))


def attention_backward(
    query_rows, key_row_block, value_rows, doc_row, denoms, grad_mixed, block_rows
):
    group_rows = query_rows.shape[0]
    grad_queries = []
    grad_keys = jnp.zeros(key_row_block.shape, jnp.float32)
    grad_values = jnp.zeros(value_rows.shape, jnp.float32)
    for row_start in range(0, group_rows, block_rows):
        row_end_index = row_start + block_rows
        score_matrix, allowed, kernel = block_kernel(
            query_rows, key_row_block, doc_row, row_start, block_rows
        )
        kernel_low = kernel.astype(jnp.bfloat16)
        denominator = denoms[:, row_start:row_end_index]
        numerator = jnp.einsum(
            "hqk,khd->qhd",
            kernel_low,
            value_rows[:row_end_index],
            preferred_element_type=jnp.float32,
        )
        grad_output = grad_mixed[row_start:row_end_index].astype(jnp.float32)
        grad_numer = (grad_output / denominator.T[:, :, None]).astype(jnp.bfloat16)
        grad_denom = -jnp.sum(grad_output * numerator, axis=-1).T / (denominator * denominator)
        grad_kernel = (
            jnp.einsum(
                "qhd,khd->hqk",
                grad_numer,
                value_rows[:row_end_index],
                preferred_element_type=jnp.float32,
            )
            + grad_denom[:, :, None]
        )
        score_gradients = jnp.where(allowed[None], grad_kernel * (1.0 + score_matrix), 0.0).astype(
            jnp.bfloat16
        )
        grad_queries.append(
            jnp.einsum(
                "zxu,uzc->xzc",
                score_gradients,
                key_row_block[:row_end_index],
                preferred_element_type=jnp.float32,
            )
            * 0.25
        )
        grad_keys = grad_keys.at[:row_end_index].add(
            jnp.einsum(
                "ari,ran->ian",
                score_gradients,
                query_rows[row_start:row_end_index],
                preferred_element_type=jnp.float32,
            )
            * 0.25
        )
        grad_values = grad_values.at[:row_end_index].add(
            jnp.einsum("hqk,qhd->khd", kernel_low, grad_numer, preferred_element_type=jnp.float32)
        )
    grad_query_rows = jnp.concatenate(grad_queries, axis=0).astype(jnp.bfloat16)
    return (grad_query_rows, grad_keys.astype(jnp.bfloat16), grad_values.astype(jnp.bfloat16))


def body(
    tokens,
    gain_one,
    w_query,
    w_key,
    w_value,
    w_out,
    gain_two,
    w_gate,
    w_up,
    w_down,
    doc_ids,
    cotangent,
):
    heads_here = w_query.shape[1] // FEAT
    doc_row = doc_ids[0]
    inputs = tokens.astype(jnp.float32)
    normed_one, scale_one, low_one = norm_rows(inputs, gain_one)
    gathered_one = lax.all_gather(low_one, "tensor", axis=0, tiled=True)
    group_rows = gathered_one.shape[0]
    block_rows = min(512, group_rows)
    query_flat = jnp.dot(gathered_one, w_query, preferred_element_type=jnp.float32).astype(
        jnp.bfloat16
    )
    key_flat = jnp.dot(gathered_one, w_key, preferred_element_type=jnp.float32).astype(jnp.bfloat16)
    value_flat = jnp.dot(gathered_one, w_value, preferred_element_type=jnp.float32).astype(
        jnp.bfloat16
    )
    query_rows = query_flat.reshape(group_rows, heads_here, FEAT)
    key_row_block = key_flat.reshape(group_rows, heads_here, FEAT)
    value_rows = value_flat.reshape(group_rows, heads_here, HEAD_V)
    mixed_blocks, denoms = attention_forward(
        query_rows, key_row_block, value_rows, doc_row, block_rows
    )
    mixed_heads = mixed_blocks.reshape(group_rows, heads_here * HEAD_V)
    part_rows = mixed_heads
    attn_out = lax.psum_scatter(
        jnp.dot(part_rows, w_out, preferred_element_type=jnp.float32),
        "tensor",
        scatter_dimension=0,
        tiled=True,
    )
    residual = inputs + attn_out
    normed_two, scale_two, low_two = norm_rows(residual, gain_two)
    gathered_two = lax.all_gather(low_two, "tensor", axis=0, tiled=True)
    gate_pre = jnp.dot(gathered_two, w_gate, preferred_element_type=jnp.float32)
    upward = jnp.dot(gathered_two, w_up, preferred_element_type=jnp.float32)
    sigmoid_gate = jax.nn.sigmoid(gate_pre)
    hidden = (gate_pre * sigmoid_gate * upward).astype(jnp.bfloat16)
    part_rows = hidden
    ffn_out = lax.psum_scatter(
        jnp.dot(part_rows, w_down, preferred_element_type=jnp.float32).astype(jnp.bfloat16),
        "tensor",
        scatter_dimension=0,
        tiled=True,
    ).astype(jnp.float32)
    block_out = (residual + ffn_out).astype(jnp.bfloat16)
    grad_rows = lax.all_gather(cotangent, "tensor", axis=0, tiled=True)
    grad_down_w = contract_rows(hidden, grad_rows)
    grad_hidden = times_transposed(grad_rows, w_down)
    slope_gate = sigmoid_gate * (1.0 + gate_pre * (1.0 - sigmoid_gate))
    grad_gate_act = (grad_hidden * upward * slope_gate).astype(jnp.bfloat16)
    grad_upward = (grad_hidden * (gate_pre * sigmoid_gate)).astype(jnp.bfloat16)
    grad_gate_w = contract_rows(gathered_two, grad_gate_act)
    grad_up_w = contract_rows(gathered_two, grad_upward)
    grad_normed_two = lax.psum_scatter(
        (times_transposed(grad_gate_act, w_gate) + times_transposed(grad_upward, w_up)).astype(
            jnp.bfloat16
        ),
        "tensor",
        scatter_dimension=0,
        tiled=True,
    ).astype(jnp.float32)
    grad_resid_norm, gain_two_part = norm_back(grad_normed_two, normed_two, scale_two, gain_two)
    grad_resid = cotangent.astype(jnp.float32) + grad_resid_norm
    grad_attn = grad_resid.astype(jnp.bfloat16)
    grad_attn_rows = lax.all_gather(grad_attn, "tensor", axis=0, tiled=True)
    grad_mixed = times_transposed(grad_attn_rows, w_out).astype(jnp.bfloat16)
    grad_out_w = contract_rows(mixed_heads, grad_attn_rows)
    grad_query_rows, grad_key_rows, grad_value_rows = attention_backward(
        query_rows,
        key_row_block,
        value_rows,
        doc_row,
        denoms,
        grad_mixed.reshape(group_rows, heads_here, HEAD_V),
        block_rows,
    )
    grad_query_flat = grad_query_rows.reshape(group_rows, heads_here * FEAT)
    grad_key_flat = grad_key_rows.reshape(group_rows, heads_here * FEAT)
    grad_value_flat = grad_value_rows.reshape(group_rows, heads_here * HEAD_V)
    grad_query_w = contract_rows(gathered_one, grad_query_flat)
    grad_key_w = contract_rows(gathered_one, grad_key_flat)
    grad_value_w = contract_rows(gathered_one, grad_value_flat)
    grad_normed_one = lax.psum_scatter(
        (
            times_transposed(grad_query_flat, w_query)
            + times_transposed(grad_key_flat, w_key)
            + times_transposed(grad_value_flat, w_value)
        ).astype(jnp.bfloat16),
        "tensor",
        scatter_dimension=0,
        tiled=True,
    ).astype(jnp.float32)
    grad_input_norm, gain_one_part = norm_back(grad_normed_one, normed_one, scale_one, gain_one)
    grad_tokens = grad_resid + grad_input_norm
    gain_grads = lax.psum((gain_one_part, gain_two_part), ("dp", "tensor"))
    weight_grads = (
        lax.psum(grad_query_w.astype(jnp.bfloat16), "dp").astype(jnp.float32),
        lax.psum(grad_key_w.astype(jnp.bfloat16), "dp").astype(jnp.float32),
        lax.psum(grad_value_w.astype(jnp.bfloat16), "dp").astype(jnp.float32),
        lax.psum(grad_out_w.astype(jnp.bfloat16), "dp").astype(jnp.float32),
        lax.psum(grad_gate_w.astype(jnp.bfloat16), "dp").astype(jnp.float32),
        lax.psum(grad_up_w.astype(jnp.bfloat16), "dp").astype(jnp.float32),
        lax.psum(grad_down_w.astype(jnp.bfloat16), "dp").astype(jnp.float32),
    )
    return (
        block_out,
        grad_tokens,
        gain_grads[0],
        weight_grads[0],
        weight_grads[1],
        weight_grads[2],
        weight_grads[3],
        gain_grads[1],
        weight_grads[4],
        weight_grads[5],
        weight_grads[6],
    )


def solution(mesh):
    in_specs = (
        P(("dp", "tensor"), None),
        P(),
        P(None, "tensor"),
        P(None, "tensor"),
        P(None, "tensor"),
        P("tensor", None),
        P(),
        P(None, "tensor"),
        P(None, "tensor"),
        P("tensor", None),
        P("dp", None),
        P(("dp", "tensor"), None),
    )
    out_specs = (
        P(("dp", "tensor"), None),
        P(("dp", "tensor"), None),
        P(),
        P(None, "tensor"),
        P(None, "tensor"),
        P(None, "tensor"),
        P("tensor", None),
        P(),
        P(None, "tensor"),
        P(None, "tensor"),
        P("tensor", None),
    )
    return jax.shard_map(body, mesh=mesh, in_specs=in_specs, out_specs=out_specs, check_vma=False)
```

profile of v0, /device:TPU:0, one launch (start us, length us, event | category | flops | bytes accessed | tf_op | source)
XLA Modules:
  0.0 1586.6 jit_solution(5318080155431390041)
XLA Ops:
  17.0 122.2 %all-gather.5.cloned.1.call-done = bf16[2048,2048]{1,0:T(8,128)(2,1)} async-done(((bf16[256,2048]{1,0:T(8,128)(2,1)}), bf16[2048,2048]{1,0:T(8,128)(2,1)}) %all-gather.5.cloned.1.call-update) | async-done | bytes 8388624 | tf_op jit(solution)/shard_map/all_gather | solution.py:155
  139.3 6.1 convolution_convert_fusion.10
  170.0 8.2 fusion.81
  178.7 280.7 %reduce-scatter.5.cloned.1.call-done = f32[256,2048]{1,0:T(8,128)} async-done(((f32[2048,2048]{1,0:T(8,128)}), f32[256,2048]{1,0:T(8,128)}) %reduce-scatter.5.cloned.1.call-update) | async-done | bytes 2097168 | tf_op jit(solution)/shard_map/reduce_scatter | solution.py:173
  464.8 123.5 %all-gather.7.cloned.1.call-done = bf16[2048,2048]{1,0:T(8,128)(2,1)} async-done(((bf16[256,2048]{1,0:T(8,128)(2,1)}), bf16[2048,2048]{1,0:T(8,128)(2,1)}) %all-gather.7.cloned.1.call-update) | async-done | bytes 8388624 | tf_op jit(solution)/shard_map/all_gather | solution.py:181
  588.3 11.2 fusion.83
  599.5 8.0 fusion.82
  607.5 106.2 %all-gather.9.cloned.1.call-done = bf16[2048,2048]{1,0:T(8,128)(2,1)} async-done(((bf16[256,2048]{1,0:T(8,128)(2,1)}), bf16[2048,2048]{1,0:T(8,128)(2,1)}) %all-gather.9.cloned.1.call-update) | async-done | bytes 8388624 | tf_op jit(solution)/shard_map/all_gather | solution.py:194
  713.7 14.6 multiply_convert_fusion
  728.3 10.5 fusion.84
  738.8 12.6 add_convert_fusion.1
  751.4 147.3 %reduce-scatter.9.cloned.1.call-done = bf16[256,2048]{1,0:T(8,128)(2,1)} async-done(((bf16[2048,2048]{1,0:T(8,128)(2,1)}), bf16[256,2048]{1,0:T(8,128)(2,1)}) %reduce-scatter.9.cloned.1.call-update) | async-done | bytes 1048592 | tf_op jit(solution)/shard_map/reduce_scatter | solution.py:202
  898.7 3.4 fusion.31
  906.1 10.9 convolution_convert_fusion.1
  917.0 10.9 convolution_convert_fusion.2
  928.0 7.8 convolution_convert_fusion.3
  935.8 94.3 %all-gather.11.cloned.1.call-done = bf16[2048,2048]{1,0:T(8,128)(2,1)} async-done(((bf16[256,2048]{1,0:T(8,128)(2,1)}), bf16[2048,2048]{1,0:T(8,128)(2,1)}) %all-gather.11.cloned.1.call-update) | async-done | bytes 8388624 | tf_op jit(solution)/shard_map/all_gather | solution.py:213
  1030.1 6.1 convolution_convert_fusion.6
  1052.1 5.1 select_convert_fusion
  1060.6 3.3 convolution_convert_fusion.4
  1066.1 3.5 convolution_convert_fusion.5
  1072.8 8.6 fusion.58
  1081.4 8.1 fusion.85
  1089.5 15.9 add_convert_fusion
  1105.4 11.0 convolution_convert_fusion
  1116.5 151.1 %all-reduce.6.cloned.1.call-done = (bf16[2048,32]{0,1:T(8,128)(2,1)}, bf16[2048,32]{0,1:T(8,128)(2,1)}, bf16[2048,256]{1,0:T(8,128)(2,1)}, bf16[256,2048]{1,0:T(...) async-done(((bf16[2048,32]{0,1:T(8,128)(2,1)}, bf16[2048,32]{0,1:T(8,128)(2,1)}, bf16[2048,256]{1,0:T(8,128)(2,1)}, ...) | async-done | bytes 11010064 | tf_op jit(solution)/shard_map/psum | solution.py:245
  1275.3 3.3 convert_element_type.237
  1282.0 3.3 convert_element_type.241
  1285.3 135.2 %reduce-scatter.11.cloned.1.call-done = bf16[256,2048]{1,0:T(8,128)(2,1)} async-done(((bf16[2048,2048]{1,0:T(8,128)(2,1)}), bf16[256,2048]{1,0:T(8,128)(2,1)}) %reduce-scatter.11.cloned.1.call-update) | async-done | bytes 1048592 | tf_op jit(solution)/shard_map/reduce_scatter | solution.py:231
  1422.9 42.8 %all-reduce.2 = (f32[2048]{0:T(1024)}, f32[2048]{0:T(1024)}) all-reduce(f32[2048]{0:T(1024)S(1)} %get-tuple-element.125, f32[2048]{0:T(1024)S(1)} %copy-done.56), channel_id=1, replica_groups=mesh['dp'=4,'tensor'=8] {'dp','tensor'}, use_global_device_ids=true, to_apply=%region_17.18 | all-reduce | flops 4096 | bytes 32768 | tf_op jit(solution)/shard_map/psum | solution.py:243
  1465.7 107.9 %reduce-scatter.7.cloned.1.call-done = bf16[256,2048]{1,0:T(8,128)(2,1)} async-done(((bf16[2048,2048]{1,0:T(8,128)(2,1)}), bf16[256,2048]{1,0:T(8,128)(2,1)}) %reduce-scatter.7.cloned.1.call-update) | async-done | bytes 1048592 | tf_op jit(solution)/shard_map/reduce_scatter | solution.py:187
  1573.7 6.0 fusion.27
  (280 shorter events, 81.3 us)
Async XLA Ops:
  7.2 706.5 %copy-start = (bf16[704,2048]{1,0:T(8,128)(2,1)S(1)}, bf16[704,2048]{1,0:T(8,128)(2,1)}, u32[]{:S(2)}) copy-start(bf16[704,2048]{1,0:T(8,128)(2,1)} %param.41) | copy-start | bytes 8650756
  7.2 132.1 %copy-start.25 = (bf16[2048,32]{0,1:T(8,128)(2,1)S(1)}, bf16[2048,32]{0,1:T(8,128)(2,1)}, u32[]{:S(2)}) copy-start(bf16[2048,32]{0,1:T(8,128)(2,1)} %param.35) | copy-start | bytes 393220
  7.2 132.0 %all-gather.5.cloned.1.call-start = ((), (), s32[]{:S(2)}) async-start(), calls=%async_computation.4 | async-start | bytes 9437184 | tf_op jit(solution)/shard_map/all_gather | solution.py:155
  11.5 447.9 %reduce-scatter.5.cloned.1.call-start = ((), (), s32[]{:S(2)}) async-start(), calls=%async_computation.5 | async-start | bytes 18874368 | tf_op jit(solution)/shard_map/reduce_scatter | solution.py:173
  13.1 142.0 %copy-start.27 = (pred[512,1024]{1,0:T(8,128)(4,1)}, pred[512,1024]{1,0:T(8,128)(4,1)S(1)}, u32[]{:S(2)}) copy-start(pred[512,1024]{1,0:T(8,128)(4,1)S(1)} %fusion.36) | copy-start | bytes 1572868
  145.4 17.2 %copy-start.11 = (bf16[2048,32]{0,1:T(8,128)(2,1)}, bf16[2048,32]{0,1:T(8,128)(2,1)S(1)}, u32[]{:S(2)}) copy-start(bf16[2048,32]{0,1:T(8,128)(2,1)S(1)} %convolution_convert_fusion.10) | copy-start | bytes 393220
  145.5 11.9 copy-start.34
  147.9 17.8 %copy-start.9 = (bf16[2048,256]{0,1:T(8,128)(2,1)}, bf16[2048,256]{0,1:T(8,128)(2,1)S(1)}, u32[]{:S(2)}) copy-start(bf16[2048,256]{0,1:T(8,128)(2,1)S(1)} %convolution_convert_fusion.7) | copy-start | bytes 3145732
  148.1 11.6 copy-start.21
  150.7 11.9 copy-start.36
  178.3 284.7 %copy-start.44 = (f32[2048]{0:T(1024)S(1)}, f32[2048]{0:T(1024)}, u32[]{:S(2)}) copy-start(f32[2048]{0:T(1024)} %param.38) | copy-start | bytes 24580
  178.3 410.0 %all-gather.7.cloned.1.call-start = ((), (), s32[]{:S(2)}) async-start(), calls=%async_computation.6 | async-start | bytes 9437184 | tf_op jit(solution)/shard_map/all_gather | solution.py:181
  461.6 440.5 %copy-start.57 = (f32[256]{0:T(256)}, f32[256]{0:T(256)S(1)}, u32[]{:S(2)}) copy-start(f32[256]{0:T(256)S(1)} %add_rsqrt_fusion) | copy-start | bytes 3076
  464.2 249.5 %all-gather.9.cloned.1.call-start = ((), (), s32[]{:S(2)}) async-start(), calls=%async_computation.8 | async-start | bytes 9437184 | tf_op jit(solution)/shard_map/all_gather | solution.py:194
  464.7 434.0 %reduce-scatter.9.cloned.1.call-start = ((), (), s32[]{:S(2)}) async-start(), calls=%async_computation.9 | async-start | bytes 9437184 | tf_op jit(solution)/shard_map/reduce_scatter | solution.py:202
  588.3 11.2 copy-start.71
  588.3 11.2 copy-start.72
  713.7 14.6 copy-start.73
  751.4 278.7 %all-gather.11.cloned.1.call-start = ((), (), s32[]{:S(2)}) async-start(), calls=%async_computation.10 | async-start | bytes 9437184 | tf_op jit(solution)/shard_map/all_gather | solution.py:213
  906.0 361.7 %all-reduce.6.cloned.1.call-start = ((), (), s32[]{:S(2)}) async-start(), calls=%async_computation.12 | async-start | bytes 22020096 | tf_op jit(solution)/shard_map/psum | solution.py:245
  906.1 21.9 %slice-start.5 = ((s8[8388608]{0:T(1024)(128)(4,1)}), s8[4194304]{0:T(1024)(128)(4,1)S(1)}, s32[]{:S(2)}) async-start(s8[8388608]{0:T(1024)(128)(4,1)} %bitcast.245), calls=%async_computation.18 | async-start | bytes 8388608
  935.8 100.6 %copy-start.70 = (f32[2,512]{1,0:T(2,128)S(1)}, f32[2,512]{1,0:T(2,128)}, u32[]{:S(2)}) copy-start(f32[2,512]{1,0:T(2,128)} %copy-done.69) | copy-start | bytes 12292
  1049.0 11.6 slice-start.3
  1052.0 14.1 copy-start.16
  1071.9 348.6 %reduce-scatter.11.cloned.1.call-start = ((), (), s32[]{:S(2)}) async-start(), calls=%async_computation.11 | async-start | bytes 9437184 | tf_op jit(solution)/shard_map/reduce_scatter | solution.py:231
  1105.4 468.3 %reduce-scatter.7.cloned.1.call-start = ((), (), s32[]{:S(2)}) async-start(), calls=%async_computation.7 | async-start | bytes 9437184 | tf_op jit(solution)/shard_map/reduce_scatter | solution.py:187
  1281.9 138.6 %copy-start.55 = (f32[2048]{0:T(1024)S(1)}, f32[2048]{0:T(1024)}, u32[]{:S(2)}) copy-start(f32[2048]{0:T(1024)} %param.33) | copy-start | bytes 24580
  1281.9 138.6 %copy-start.60 = (f32[256]{0:T(256)S(1)}, f32[256]{0:T(256)}, u32[]{:S(2)}) copy-start(f32[256]{0:T(256)} %copy-done.59) | copy-start | bytes 3076
  1281.9 140.9 %copy-start.56 = (f32[2048]{0:T(1024)S(1)}, f32[2048]{0:T(1024)}, u32[]{:S(2)}) copy-start(f32[2048]{0:T(1024)} %get-tuple-element.123) | copy-start | bytes 24580
  1282.0 291.7 %copy-start.45 = (f32[2048]{0:T(1024)S(1)}, f32[2048]{0:T(1024)}, u32[]{:S(2)}) copy-start(f32[2048]{0:T(1024)} %param.38) | copy-start | bytes 24580
  1282.0 291.7 %copy-start.58 = (f32[256]{0:T(256)S(1)}, f32[256]{0:T(256)}, u32[]{:S(2)}) copy-start(f32[256]{0:T(256)} %copy-done.57) | copy-start | bytes 3076
  1282.0 291.7 %copy-start.62 = (f32[256]{0:T(256)S(1)}, f32[256]{0:T(256)}, u32[]{:S(2)}) copy-start(f32[256]{0:T(256)} %copy-done.61) | copy-start | bytes 3076
  (73 other events, 285.9 us)
Sparse Core Ops, SparseCore 0:
  11.6 127.6 all-gather.4
  178.4 280.9 reduce-scatter.4
  464.3 123.9 all-gather.6
  590.5 123.1 all-gather.8
  751.5 147.1 reduce-scatter.8
  906.1 123.9 all-gather.10
  1072.0 195.5 all-reduce.5
  1271.3 149.1 reduce-scatter.10
  1424.6 149.0 reduce-scatter.6
where the time goes:
time: 1600 us; the launch traced here: 1590 us
  waiting for transfers between devices  1270 us (79%)
  matrix products  205 us (13%)
  other arithmetic  46.1 us (3%)
  blocking collectives  42.8 us (3%)
    reduce_scatter x1, waiting for transfers between devices, body(): lax.psum_scatter(jnp.dot(part_rows, w_out, preferred_element_type=jnp.flo...  281 us
    psum x1, waiting for transfers between devices, body(): lax.psum(grad_query_w.astype(jnp.bfloat16), 'dp').astype(jnp.float32)  151 us
    reduce_scatter x1, waiting for transfers between devices, body(): lax.psum_scatter((times_transposed(grad_gate_act, w_gate) + times_transpo...  147 us
    reduce_scatter x1, waiting for transfers between devices, body(): lax.psum_scatter((times_transposed(grad_query_flat, w_query) + times_tran...  135 us
    all_gather x1, waiting for transfers between devices, body(): gathered_two = lax.all_gather(low_two, 'tensor', axis=0, tiled=True)  124 us
    all_gather x1, waiting for transfers between devices, body(): gathered_one = lax.all_gather(low_one, 'tensor', axis=0, tiled=True)  122 us
    reduce_scatter x1, waiting for transfers between devices, body(): lax.psum_scatter(jnp.dot(part_rows, w_down, preferred_element_type=jnp.fl...  108 us
    all_gather x1, waiting for transfers between devices, body(): grad_rows = lax.all_gather(cotangent, 'tensor', axis=0, tiled=True)  106 us
  transfers between devices with their start and end apart: 9, of which 9 were waited for; matrix products, arithmetic and copies ran while one was open for 7% of the time, Pallas kernels for 0%

commit v1 on v0

--- a/solution.py
+++ b/solution.py
@@ -242,7 +242,9 @@
     grad_tokens = grad_resid + grad_input_norm
     gain_grads = lax.psum((gain_one_part, gain_two_part), ("dp", "tensor"))
     weight_grads = (
-        lax.psum(grad_query_w.astype(jnp.bfloat16), "dp").astype(jnp.float32),
+        jnp.sum(lax.all_gather(grad_query_w.astype(jnp.bfloat16), "dp"), axis=0).astype(
+            jnp.float32
+        ),
         lax.psum(grad_key_w.astype(jnp.bfloat16), "dp").astype(jnp.float32),
         lax.psum(grad_value_w.astype(jnp.bfloat16), "dp").astype(jnp.float32),
         lax.psum(grad_out_w.astype(jnp.bfloat16), "dp").astype(jnp.float32),

time: 1600 us -> 1600 us (level)
  waiting for transfers between devices: 1270 us -> 1240 us
    psum x1, waiting for transfers between devices: 151 us -> 125 us  [body(): lax.psum(grad_key_w.astype(jnp.bfloat16), 'dp').astype(jnp.float32)]
  transfers between devices with their start and end apart: 9 -> 9, of which waited for: 9 -> 9; matrix products, arithmetic and copies ran while one was open for 7% -> 8% of each run, Pallas kernels for 0% -> 0%
where the time goes in v1:
time: 1600 us; the launch traced here: 1590 us
  waiting for transfers between devices  1240 us (78%)
  matrix products  217 us (14%)
  blocking collectives  53.1 us (3%)
  other arithmetic  48.1 us (3%)
    reduce_scatter x1, waiting for transfers between devices, body(): lax.psum_scatter(jnp.dot(part_rows, w_out, preferred_element_type=jnp.flo...  281 us
    reduce_scatter x1, waiting for transfers between devices, body(): lax.psum_scatter((times_transposed(grad_gate_act, w_gate) + times_transpo...  147 us
    reduce_scatter x1, waiting for transfers between devices, body(): lax.psum_scatter((times_transposed(grad_query_flat, w_query) + times_tran...  136 us
    psum x1, waiting for transfers between devices, body(): lax.psum(grad_key_w.astype(jnp.bfloat16), 'dp').astype(jnp.float32)  125 us
    all_gather x1, waiting for transfers between devices, body(): gathered_two = lax.all_gather(low_two, 'tensor', axis=0, tiled=True)  123 us
    all_gather x1, waiting for transfers between devices, body(): gathered_one = lax.all_gather(low_one, 'tensor', axis=0, tiled=True)  122 us
    reduce_scatter x1, waiting for transfers between devices, body(): lax.psum_scatter(jnp.dot(part_rows, w_down, preferred_element_type=jnp.fl...  108 us
    all_gather x1, waiting for transfers between devices, body(): grad_rows = lax.all_gather(cotangent, 'tensor', axis=0, tiled=True)  106 us
  transfers between devices with their start and end apart: 9, of which 9 were waited for; matrix products, arithmetic and copies ran while one was open for 8% of the time, Pallas kernels for 0%

profile of v1, /device:TPU:0, one launch (start us, length us, event | category | flops | bytes accessed | tf_op | source)
XLA Modules:
  0.0 1588.7 jit_solution(12275706734646773396)
XLA Ops:
  17.0 122.2 %all-gather.6.cloned.1.call-done = bf16[2048,2048]{1,0:T(8,128)(2,1)} async-done(((bf16[256,2048]{1,0:T(8,128)(2,1)}), bf16[2048,2048]{1,0:T(8,128)(2,1)}) %all-gather.6.cloned.1.call-update) | async-done | bytes 8388624 | tf_op jit(solution)/shard_map/all_gather | solution.py:155
  139.3 6.1 convolution_convert_fusion.10
  170.0 8.2 fusion.81
  178.5 280.8 %reduce-scatter.5.cloned.1.call-done = f32[256,2048]{1,0:T(8,128)} async-done(((f32[2048,2048]{1,0:T(8,128)}), f32[256,2048]{1,0:T(8,128)}) %reduce-scatter.5.cloned.1.call-update) | async-done | bytes 2097168 | tf_op jit(solution)/shard_map/reduce_scatter | solution.py:173
  464.7 123.5 %all-gather.8.cloned.1.call-done = bf16[2048,2048]{1,0:T(8,128)(2,1)} async-done(((bf16[256,2048]{1,0:T(8,128)(2,1)}), bf16[2048,2048]{1,0:T(8,128)(2,1)}) %all-gather.8.cloned.1.call-update) | async-done | bytes 8388624 | tf_op jit(solution)/shard_map/all_gather | solution.py:181
  588.2 11.2 fusion.83
  599.3 8.0 fusion.82
  607.3 106.2 %all-gather.10.cloned.1.call-done = bf16[2048,2048]{1,0:T(8,128)(2,1)} async-done(((bf16[256,2048]{1,0:T(8,128)(2,1)}), bf16[2048,2048]{1,0:T(8,128)(2,1)}) %all-gather.10.cloned.1.call-update) | async-done | bytes 8388624 | tf_op jit(solution)/shard_map/all_gather | solution.py:194
  713.5 14.6 multiply_convert_fusion
  728.2 10.9 fusion.84
  739.0 12.5 add_convert_fusion.1
  751.6 147.3 %reduce-scatter.9.cloned.1.call-done = bf16[256,2048]{1,0:T(8,128)(2,1)} async-done(((bf16[2048,2048]{1,0:T(8,128)(2,1)}), bf16[256,2048]{1,0:T(8,128)(2,1)}) %reduce-scatter.9.cloned.1.call-update) | async-done | bytes 1048592 | tf_op jit(solution)/shard_map/reduce_scatter | solution.py:202
  898.9 3.4 fusion.31
  906.2 10.8 convolution_convert_fusion.1
  917.1 11.0 convolution_convert_fusion.2
  928.1 7.7 convolution_convert_fusion.3
  935.7 94.5 %all-gather.12.cloned.1.call-done = bf16[2048,2048]{1,0:T(8,128)(2,1)} async-done(((bf16[256,2048]{1,0:T(8,128)(2,1)}), bf16[2048,2048]{1,0:T(8,128)(2,1)}) %all-gather.12.cloned.1.call-update) | async-done | bytes 8388624 | tf_op jit(solution)/shard_map/all_gather | solution.py:213
  1030.2 6.1 convolution_convert_fusion.6
  1049.9 7.2 fusion.16
  1057.2 5.1 select_convert_fusion
  1070.4 3.5 convolution_convert_fusion.5
  1082.9 8.2 fusion.58
  1091.1 8.2 fusion.85
  1099.2 15.8 add_convert_fusion
  1115.1 10.9 convolution_convert_fusion
  1126.0 5.0 convolution_convert_fusion.9
  1131.0 10.7 all-gather
  1145.3 124.7 %all-reduce.6.cloned.1.call-done = (bf16[2048,32]{0,1:T(8,128)(2,1)}, bf16[2048,256]{1,0:T(8,128)(2,1)}, bf16[256,2048]{1,0:T(8,128)(2,1)}, bf16[2048,704]{0,1:T...) async-done(((bf16[2048,32]{0,1:T(8,128)(2,1)}, bf16[2048,256]{1,0:T(8,128)(2,1)}, bf16[256,2048]{1,0:T(8,128)(2,1)}, bf16[2048,704]{0,1:T(8,128)(2,1)}, ...) | async-done | bytes 10878992 | tf_op jit(solution)/shard_map/psum | solution.py:248
  1287.4 135.9 %reduce-scatter.11.cloned.1.call-done = bf16[256,2048]{1,0:T(8,128)(2,1)} async-done(((bf16[2048,2048]{1,0:T(8,128)(2,1)}), bf16[256,2048]{1,0:T(8,128)(2,1)}) %reduce-scatter.11.cloned.1.call-update) | async-done | bytes 1048592 | tf_op jit(solution)/shard_map/reduce_scatter | solution.py:231
  1425.7 42.4 %all-reduce.2 = (f32[2048]{0:T(1024)}, f32[2048]{0:T(1024)}) all-reduce(f32[2048]{0:T(1024)S(1)} %get-tuple-element.125, f32[2048]{0:T(1024)S(1)} %copy-done.60), channel_id=1, replica_groups=mesh['dp'=4,'tensor'=8] {'dp','tensor'}, use_global_device_ids=true, to_apply=%region_17.18 | all-reduce | flops 4096 | bytes 32768 | tf_op jit(solution)/shard_map/psum | solution.py:243
  1468.1 107.8 %reduce-scatter.7.cloned.1.call-done = bf16[256,2048]{1,0:T(8,128)(2,1)} async-done(((bf16[2048,2048]{1,0:T(8,128)(2,1)}), bf16[256,2048]{1,0:T(8,128)(2,1)}) %reduce-scatter.7.cloned.1.call-update) | async-done | bytes 1048592 | tf_op jit(solution)/shard_map/reduce_scatter | solution.py:187
  1575.9 6.0 fusion.27
  (282 shorter events, 97.1 us)
Async XLA Ops:
  7.2 706.3 %copy-start = (bf16[704,2048]{1,0:T(8,128)(2,1)S(1)}, bf16[704,2048]{1,0:T(8,128)(2,1)}, u32[]{:S(2)}) copy-start(bf16[704,2048]{1,0:T(8,128)(2,1)} %param.41) | copy-start | bytes 8650756
  7.2 132.1 %copy-start.29 = (bf16[2048,32]{0,1:T(8,128)(2,1)S(1)}, bf16[2048,32]{0,1:T(8,128)(2,1)}, u32[]{:S(2)}) copy-start(bf16[2048,32]{0,1:T(8,128)(2,1)} %param.35) | copy-start | bytes 393220
  7.2 132.0 %all-gather.6.cloned.1.call-start = ((), (), s32[]{:S(2)}) async-start(), calls=%async_computation.4 | async-start | bytes 9437184 | tf_op jit(solution)/shard_map/all_gather | solution.py:155
  11.5 447.8 %reduce-scatter.5.cloned.1.call-start = ((), (), s32[]{:S(2)}) async-start(), calls=%async_computation.5 | async-start | bytes 18874368 | tf_op jit(solution)/shard_map/reduce_scatter | solution.py:173
  13.1 142.0 %copy-start.31 = (pred[512,1024]{1,0:T(8,128)(4,1)}, pred[512,1024]{1,0:T(8,128)(4,1)S(1)}, u32[]{:S(2)}) copy-start(pred[512,1024]{1,0:T(8,128)(4,1)S(1)} %fusion.36) | copy-start | bytes 1572868
  145.4 17.2 %copy-start.16 = (bf16[2048,32]{0,1:T(8,128)(2,1)}, bf16[2048,32]{0,1:T(8,128)(2,1)S(1)}, u32[]{:S(2)}) copy-start(bf16[2048,32]{0,1:T(8,128)(2,1)S(1)} %convolution_convert_fusion.10) | copy-start | bytes 393220
  145.5 11.9 copy-start.38
  147.9 17.7 %copy-start.14 = (bf16[2048,256]{0,1:T(8,128)(2,1)}, bf16[2048,256]{0,1:T(8,128)(2,1)S(1)}, u32[]{:S(2)}) copy-start(bf16[2048,256]{0,1:T(8,128)(2,1)S(1)} %convolution_convert_fusion.7) | copy-start | bytes 3145732
  148.1 11.6 copy-start.25
  150.7 11.8 copy-start.40
  178.2 284.6 %copy-start.48 = (f32[2048]{0:T(1024)S(1)}, f32[2048]{0:T(1024)}, u32[]{:S(2)}) copy-start(f32[2048]{0:T(1024)} %param.38) | copy-start | bytes 24580
  178.2 409.9 %all-gather.8.cloned.1.call-start = ((), (), s32[]{:S(2)}) async-start(), calls=%async_computation.6 | async-start | bytes 9437184 | tf_op jit(solution)/shard_map/all_gather | solution.py:181
  461.5 440.8 %copy-start.61 = (f32[256]{0:T(256)}, f32[256]{0:T(256)S(1)}, u32[]{:S(2)}) copy-start(f32[256]{0:T(256)S(1)} %add_rsqrt_fusion) | copy-start | bytes 3076
  464.1 249.4 %all-gather.10.cloned.1.call-start = ((), (), s32[]{:S(2)}) async-start(), calls=%async_computation.8 | async-start | bytes 9437184 | tf_op jit(solution)/shard_map/all_gather | solution.py:194
  464.7 434.3 %reduce-scatter.9.cloned.1.call-start = ((), (), s32[]{:S(2)}) async-start(), calls=%async_computation.9 | async-start | bytes 9437184 | tf_op jit(solution)/shard_map/reduce_scatter | solution.py:202
  713.5 14.6 copy-start.75
  751.6 278.7 %all-gather.12.cloned.1.call-start = ((), (), s32[]{:S(2)}) async-start(), calls=%async_computation.10 | async-start | bytes 9437184 | tf_op jit(solution)/shard_map/all_gather | solution.py:213
  906.1 363.9 %all-reduce.6.cloned.1.call-start = ((), (), s32[]{:S(2)}) async-start(), calls=%async_computation.12 | async-start | bytes 21757952 | tf_op jit(solution)/shard_map/psum | solution.py:248
  906.2 21.8 %slice-start.5 = ((s8[8388608]{0:T(1024)(128)(4,1)}), s8[4194304]{0:T(1024)(128)(4,1)S(1)}, s32[]{:S(2)}) async-start(s8[8388608]{0:T(1024)(128)(4,1)} %bitcast.247), calls=%async_computation.18 | async-start | bytes 8388608
  935.7 100.8 %copy-start.72 = (f32[2,512]{1,0:T(2,128)S(1)}, f32[2,512]{1,0:T(2,128)}, u32[]{:S(2)}) copy-start(f32[2,512]{1,0:T(2,128)} %copy-done.71) | copy-start | bytes 12292
  1042.4 20.0 %copy-start.7 = (bf16[2,512,1024]{2,1,0:T(8,128)(2,1)}, bf16[2,512,1024]{2,1,0:T(8,128)(2,1)S(1)}, u32[]{:S(2)}) copy-start(bf16[2,512,1024]{2,1,0:T(8,128)(2,1)S(1)} %select_convert_fusion.2) | copy-start | bytes 6291460
  1049.9 12.9 copy-start.6
  1049.9 14.5 slice-start.3
  1057.1 13.2 copy-start.20
  1074.0 349.3 %reduce-scatter.11.cloned.1.call-start = ((), (), s32[]{:S(2)}) async-start(), calls=%async_computation.11 | async-start | bytes 9437184 | tf_op jit(solution)/shard_map/reduce_scatter | solution.py:231
  1115.0 460.9 %reduce-scatter.7.cloned.1.call-start = ((), (), s32[]{:S(2)}) async-start(), calls=%async_computation.7 | async-start | bytes 9437184 | tf_op jit(solution)/shard_map/reduce_scatter | solution.py:187
  1284.0 139.3 %copy-start.59 = (f32[2048]{0:T(1024)S(1)}, f32[2048]{0:T(1024)}, u32[]{:S(2)}) copy-start(f32[2048]{0:T(1024)} %param.33) | copy-start | bytes 24580
  1284.0 139.3 %copy-start.64 = (f32[256]{0:T(256)S(1)}, f32[256]{0:T(256)}, u32[]{:S(2)}) copy-start(f32[256]{0:T(256)} %copy-done.63) | copy-start | bytes 3076
  1284.0 141.7 %copy-start.60 = (f32[2048]{0:T(1024)S(1)}, f32[2048]{0:T(1024)}, u32[]{:S(2)}) copy-start(f32[2048]{0:T(1024)} %get-tuple-element.123) | copy-start | bytes 24580
  1284.0 291.9 %copy-start.49 = (f32[2048]{0:T(1024)S(1)}, f32[2048]{0:T(1024)}, u32[]{:S(2)}) copy-start(f32[2048]{0:T(1024)} %param.38) | copy-start | bytes 24580
  1284.0 291.9 %copy-start.62 = (f32[256]{0:T(256)S(1)}, f32[256]{0:T(256)}, u32[]{:S(2)}) copy-start(f32[256]{0:T(256)} %copy-done.61) | copy-start | bytes 3076
  1284.0 291.9 %copy-start.66 = (f32[256]{0:T(256)S(1)}, f32[256]{0:T(256)}, u32[]{:S(2)}) copy-start(f32[256]{0:T(256)} %copy-done.65) | copy-start | bytes 3076
  (73 other events, 320.4 us)
Sparse Core Ops, SparseCore 0:
  11.6 127.6 all-gather.5
  178.4 280.8 reduce-scatter.4
  464.2 123.9 all-gather.7
  590.4 123.1 all-gather.9
  751.7 147.1 reduce-scatter.8
  906.3 123.9 all-gather.11
  1074.1 195.8 all-reduce.5
  1274.1 149.1 reduce-scatter.10
  1426.9 148.9 reduce-scatter.6
